TPU v7x, 32 devices: a whole 2x2x4 slice. The times are simulated.
32 devices in a mesh: fibre: 8 (over z, x), day: 4 (over y, core).
Axes of the slice: x: 2, y: 2, z: 4, core: 2. Of those that a mesh axis runs over, the one named last changes fastest.
Arguments:
- raw_strain: bfloat16 [4, 48, 1024, 512], P('day', None, 'fibre'), may hold values from -6 to 6
- gain_index: int32 [1024], P('fibre'), may hold values from 0 to 7
- dead_mask: int32 [1024], P('fibre'), may hold values 0 or 1
- gain_table: float32 [8], replicated, may hold values from 0.5 to 2
- source_index: int32 [4, 16], replicated, may hold values from 0 to 1023, as said below
Outputs:
- correlations: float32 [64, 1024, 256], P('day', 'fibre')
Inputs may be any that keep to these rules, and one draw needn't show every extreme that they name: `source_index`: the 16 channels of a row are different and all lie in one aligned run of 128 channels, numbers k * 128 .. (k + 1) * 128 - 1. The first row lies in the first run and holds channel 0, the last row lies in the last run and holds the fibre's last channel; the run of each other row is drawn.
All inputs are finite; a program needn't handle non-finite values. No bound on the sum of `dead_mask` on one device may be relied on, other than what follows from the above.
Results may differ from a plain program's by a relative error of at most 0.0019.
Values may be sent and summed in bfloat16 or wider, within the bound.
A program may use at most 128 MiB of HBM per device.

v0:
```python
import math
import jax
import jax.numpy as jnp
from jax import lax
from jax.sharding import PartitionSpec as P

HALF = 16


def with_halo(block, sides, width):
    for axis, dim in sides:
        count = lax.axis_size(axis)
        forward = [(i, i + 1) for i in range(count - 1)]
        backward = [(target, source) for source, target in forward]
        low = lax.ppermute(
            lax.slice_in_dim(block, block.shape[dim] - width, None, axis=dim), axis, forward
        )
        high = lax.ppermute(lax.slice_in_dim(block, 0, width, axis=dim), axis, backward)
        block = jnp.concatenate([low, block, high], axis=dim)
    return block


def entering(part, axis, combine, identity):
    place = lax.axis_index(axis)
    gathered = lax.all_gather(part, axis)
    state = jnp.zeros_like(part) + jnp.asarray(identity, part.dtype)

    def one(step, state):
        return combine(state, lax.dynamic_index_in_dim(gathered, step, 0, False))

    return lax.fori_loop(0, place, one, state)


def dft_table(length, bin_count):
    times = jnp.arange(length, dtype=jnp.int32)
    freqs = jnp.arange(bin_count, dtype=jnp.int32)
    phase = (times[:, None] * freqs[None, :] % length).astype(jnp.float32) * (
        2.0 * math.pi / length
    )
    taper = 0.5 - 0.5 * jnp.cos(times.astype(jnp.float32) * (2.0 * math.pi / length))
    table = jnp.concatenate(
        [taper[:, None] * jnp.cos(phase), -taper[:, None] * jnp.sin(phase)], axis=1
    )
    return table.astype(jnp.bfloat16)


def band_table(bin_count, reach):
    first = jnp.arange(bin_count, dtype=jnp.int32)
    near_bins = (jnp.abs(first[:, None] - first[None, :]) <= reach).astype(jnp.float32)
    counts = jnp.sum(near_bins, axis=0)
    return near_bins / counts[None, :]


def lag_table(length, bin_count, lag_count):
    freqs = jnp.arange(bin_count, dtype=jnp.int32)
    lag_vals = jnp.arange(lag_count, dtype=jnp.int32) - lag_count // 2
    phase = (freqs[:, None] * lag_vals[None, :] % length).astype(jnp.float32) * (
        2.0 * math.pi / length
    )
    weight = jnp.where(freqs == 0, 1.0, 2.0).astype(jnp.float32) / length
    return jnp.concatenate(
        [weight[:, None] * jnp.cos(phase), -weight[:, None] * jnp.sin(phase)], axis=0
    )


def add_terms(earlier, later):
    return earlier + later


def per_device(raw_strain, gain_index, dead_mask, gain_table, source_index):
    seg_count = raw_strain.shape[1]
    chan_count = raw_strain.shape[2]
    length = raw_strain.shape[3]
    bin_count = length // 2
    reach = HALF
    settings = jnp.arange(gain_table.shape[0], dtype=jnp.int32)
    onehot_gain = (gain_index[:, None] == settings[None, :]).astype(jnp.float32)
    channel_gain = jnp.sum(onehot_gain * gain_table[None, :], axis=1) * dead_mask.astype(
        jnp.float32
    )
    calibrated = (raw_strain[0].astype(jnp.float32) * channel_gain[None, :, None]).astype(
        jnp.bfloat16
    )
    padded = with_halo(calibrated, (("fibre", 1),), reach)
    rows_here = jnp.arange(chan_count, dtype=jnp.int32)
    cols_here = jnp.arange(chan_count + 2 * reach, dtype=jnp.int32)
    offset_grid = cols_here[None, :] - rows_here[:, None]
    band_ones = ((offset_grid >= 0) & (offset_grid <= 2 * reach)).astype(jnp.bfloat16)
    window = jnp.einsum("ck,skl->scl", band_ones, padded, preferred_element_type=jnp.float32)
    detrended = calibrated.astype(jnp.float32) - window / (2 * reach + 1)
    local_cum = jnp.cumsum(detrended, axis=1)
    carried = entering(
        local_cum[:, -1, :], "fibre", add_terms, jnp.zeros((seg_count, length), jnp.float32)
    )
    displacement = (local_cum + carried[:, None, :]).astype(jnp.bfloat16)
    spectra = jnp.dot(
        displacement.reshape(-1, length),
        dft_table(length, bin_count),
        preferred_element_type=jnp.float32,
    )
    real_part = spectra[:, :bin_count]
    imag_part = spectra[:, bin_count:]
    power_bins = real_part * real_part + imag_part * imag_part
    smooth = jnp.dot(
        power_bins, band_table(bin_count, bin_count // 4), precision=lax.Precision.HIGHEST
    )
    inv_amp = lax.rsqrt(smooth + 1e-06)
    whitened = (spectra * jnp.concatenate([inv_amp, inv_amp], axis=1)).astype(jnp.bfloat16)
    whitened = whitened.reshape(seg_count, chan_count, length)
    own_index = lax.axis_index("fibre")
    block_count = source_index.shape[0]
    offered = []
    for block in range(block_count):
        holder = source_index[block, 0] // chan_count
        local_rows = jnp.clip(source_index[block] - own_index * chan_count, 0, chan_count - 1)
        offered.append(
            jnp.where(
                holder == own_index,
                jnp.take(whitened, local_rows, axis=1),
                jnp.zeros((), jnp.bfloat16),
            )
        )
    offered_all = jnp.concatenate(offered, axis=1).astype(jnp.float32)
    sources = lax.psum(offered_all.astype(jnp.bfloat16), "fibre")
    chan_re = whitened[:, :, :bin_count]
    chan_im = whitened[:, :, bin_count:]
    inverse = lag_table(length, bin_count, bin_count)
    day_count = lax.axis_size("day")
    src_re = sources[:, :, :bin_count]
    src_im = sources[:, :, bin_count:]
    real_sum = jnp.einsum("gsf,gcf->scf", src_re, chan_re, preferred_element_type=jnp.float32)
    real_sum = real_sum + jnp.einsum(
        "gsf,gcf->scf", src_im, chan_im, preferred_element_type=jnp.float32
    )
    imag_sum = jnp.einsum("gsf,gcf->scf", src_im, chan_re, preferred_element_type=jnp.float32)
    imag_sum = imag_sum - jnp.einsum(
        "gsf,gcf->scf", src_re, chan_im, preferred_element_type=jnp.float32
    )
    stacked = lax.psum_scatter(
        jnp.einsum(
            "scm,mj->scj",
            jnp.concatenate([real_sum, imag_sum], axis=2),
            inverse,
            precision=lax.Precision.HIGHEST,
        ),
        "day",
        scatter_dimension=0,
        tiled=True,
    )
    return stacked * (1.0 / (seg_count * day_count))


def solution(mesh):
    return jax.shard_map(
        per_device,
        mesh=mesh,
        in_specs=(P("day", None, "fibre", None), P("fibre"), P("fibre"), P(), P()),
        out_specs=P("day", "fibre", None),
        check_vma=False,
    )
```

profile of v0, /device:TPU:0, one launch (start us, length us, event | category | flops | bytes accessed | tf_op | source)
XLA Modules:
  0.0 450.3 jit_solution(5346271762334329487)
XLA Ops:
  8.0 5.0 %fusion.3 = bf16[48,128,512]{2,1,0:T(8,128)(2,1)S(1)} fusion(bf16[1,48,128,512]{3,2,1,0:T(8,128)(2,1)} %param.9, f32[128]{0:T(128)S(1)} %convert_multiply_fusion.1), kind=kLoop, calls=%fused_computation.11 | loop fusion | flops 9437184 | bytes 12583424 | tf_op jit(solution)/shard_map/convert_element_type | solution.py:81
  13.0 2.7 copy-done.3
  15.8 4.9 %collective-permute-start = (bf16[48,16,512]{2,1,0:T(8,128)(2,1)S(1)}, bf16[48,16,512]{2,1,0:T(8,128)(2,1)S(1)}, u32[]{:S(2)}, u32[]{:S(2)}) collective-permute-start(bf16[48,16,512]{2,1,0:T(8,128)(2,1)S(1)} %get-tuple-element.48), channel_id=1, source_target_pairs={{0,4},{4,8},{8,12},{12,16},{16,20},{20,24},{24,28},{1,5},{5,9},{9,... | collective-permute-start | bytes 2359304 | tf_op jit(solution)/shard_map/ppermute | solution.py:15
  33.1 3.0 multiply_convert_fusion
  36.1 18.1 %collective-permute-done = bf16[48,16,512]{2,1,0:T(8,128)(2,1)S(1)} collective-permute-done((bf16[48,16,512]{2,1,0:T(8,128)(2,1)S(1)}, bf16[48,16,512]{2,1,0:T(8,128)(2,1)S(1)}, u32[]{:S(2)}, u32[]{:S(2)}) %collective-permute-start) | collective-permute-done | bytes 786464 | tf_op jit(solution)/shard_map/ppermute | solution.py:15
  54.3 8.5 %bitcast_subtract_fusion = f32[48,128,512]{2,1,0:T(8,128)} fusion(bf16[48,128,512]{2,1,0:T(8,128)(2,1)} %copy-done.3, bf16[48,16,512]{2,1,0:T(8,128)(2,1)S(1)} %collective-permute-done.1, bf16[48,16,512]{2,1,0:T(8,128)(2,1)S(1)} %collective-permute-done), kind=kOutput, calls=%fused_computation.12 | convolution fusion | flops 1039745024 | bytes 20447232 | tf_op jit(solution)/shard_map/ck,skl->scl/dot_general | solution.py:89
  62.8 15.4 %fusion.4 = f32[48,128,512]{2,0,1:T(8,128)} fusion(f32[48,128,512]{2,1,0:T(8,128)} %bitcast_subtract_fusion), kind=kOutput, calls=%fused_computation.13 | output fusion | flops 399507456 | bytes 25165824 | tf_op jit(solution)/shard_map/jit(cumsum)/reduce_window_sum | solution.py:91
  79.0 34.4 %all-gather = f32[384,1,512]{2,0,1:T(8,128)S(1)} all-gather(f32[48,1,512]{2,0,1:T(8,128)S(1)} %slice.78), channel_id=2, replica_groups=mesh['fibre'=8,'day'=4] {'fibre'}, dimensions={0}, use_global_device_ids=true | all-gather | bytes 884736 | tf_op jit(solution)/shard_map/all_gather | solution.py:25
  113.7 6.6 %add_convert_fusion = bf16[48,128,512]{2,0,1:T(8,128)(2,1)S(1)} fusion(f32[48,128,512]{2,0,1:T(8,128)} %fusion.4, f32[48,512]{1,0:T(8,128)S(1)} %get-tuple-element.29), kind=kLoop, calls=%fused_computation.15 | loop fusion | flops 6291456 | bytes 18972672 | tf_op jit(solution)/shard_map/convert_element_type | solution.py:95
  120.3 3.6 copy.42
  123.9 4.4 fusion.20
  128.3 5.7 %fusion.6 = f32[6144,256]{1,0:T(8,128)S(1)} fusion(f32[6144,512]{1,0:T(8,128)S(1)} %fusion.20, f32[256]{0:T(256)S(1)} %convert_reduce_fusion), kind=kOutput, calls=%fused_computation.19 | convolution fusion | flops 4838457344 | bytes 18875392 | tf_op jit(solution)/shard_map/dot_general | solution.py:104
  134.0 2.0 fusion.2
  136.1 6.3 %copy.45 = bf16[48,128,512]{2,0,1:T(8,128)(2,1)} copy(bf16[48,128,512]{2,1,0:T(8,128)(2,1)S(1)} %bitcast.55) | data formatting | bytes 12582912 | tf_op jit(solution)/shard_map/reshape | solution.py:109
  142.4 3.4 gather_fusion.3
  145.8 3.4 gather_fusion.2
  149.2 3.4 gather_fusion.1
  152.5 3.4 gather_fusion
  160.6 5.3 %fusion.54 = (bf16[48,128,256]{2,1,0:T(8,128)(2,1)S(1)}, bf16[48,128,256]{2,1,0:T(8,128)(2,1)}) fusion(bf16[48,128,512]{2,1,0:T(8,128)(2,1)} %bitcast.56), kind=kLoop, calls=%fused_computation.103 | loop fusion | bytes 12582912 | tf_op jit(solution)/shard_map/slice | solution.py:126
  165.9 4.9 %copy.57 = bf16[48,128,256]{1,0,2:T(8,128)(2,1)} copy(bf16[48,128,256]{2,1,0:T(8,128)(2,1)} %get-tuple-element.47) | data formatting | bytes 6291456
  170.9 3.4 copy.58
  174.3 112.3 %all-reduce.2.cloned.1.call-done = bf16[48,64,512]{2,0,1:T(8,128)(2,1)} async-done(((bf16[48,64,512]{2,0,1:T(8,128)(2,1)}), bf16[48,64,512]{2,0,1:T(8,128)(2,1)}) %all-reduce.2.cloned.1.call-update) | async-done | bytes 3145744 | tf_op jit(solution)/shard_map/psum | solution.py:124
  286.6 2.1 fusion.56
  288.7 4.8 %copy.49 = bf16[48,64,256]{1,0,2:T(8,128)(2,1)} copy(bf16[48,64,256]{2,0,1:T(8,128)(2,1)S(1)} %get-tuple-element.50) | data formatting | bytes 3145728 | tf_op jit(solution)/shard_map/slice | solution.py:129
  293.5 4.9 %copy.51 = bf16[48,64,256]{1,0,2:T(8,128)(2,1)} copy(bf16[48,64,256]{2,0,1:T(8,128)(2,1)S(1)} %get-tuple-element.51) | data formatting | bytes 3145728 | tf_op jit(solution)/shard_map/slice | solution.py:130
  298.5 4.3 fusion.58
  304.5 7.6 %add_bitcast_fusion = f32[64,128,256]{1,0,2:T(8,128)} fusion(f32[256,128,64]{1,2,0:T(8,128)S(1)} %fusion.58, bf16[48,128,256]{1,0,2:T(8,128)(2,1)} %copy.58, bf16[48,64,256]{1,0,2:T(8,128)(2,1)} %copy.51), kind=kOutput, calls=%fused_computation.17 | convolution fusion | flops 203423744 | bytes 21495808 | tf_op jit(solution)/shard_map/gsf,gcf->scf/dot_general | solution.py:132
  312.1 7.6 %subtract_bitcast_fusion = f32[64,128,256]{1,0,2:T(8,128)} fusion(f32[256,128,64]{1,2,0:T(8,128)S(1)} %fusion.59, bf16[48,128,256]{1,0,2:T(8,128)(2,1)} %copy.58, bf16[48,64,256]{1,0,2:T(8,128)(2,1)} %copy.49), kind=kOutput, calls=%fused_computation.16 | convolution fusion | flops 203423744 | bytes 21495808 | tf_op jit(solution)/shard_map/gsf,gcf->scf/dot_general | solution.py:136
  319.6 7.2 %pad_maximum_fusion = f32[64,128,512]{1,0,2:T(8,128)S(1)} fusion(f32[64,128,256]{1,0,2:T(8,128)} %subtract_bitcast_fusion, f32[64,128,256]{1,0,2:T(8,128)} %add_bitcast_fusion), kind=kLoop, calls=%fused_computation.5 | loop fusion | flops 4194304 | bytes 33554432 | tf_op jit(solution)/shard_map/concatenate | solution.py:142
  326.8 42.3 %fusion = f32[64,128,256]{2,1,0:T(8,128)} fusion(f32[64,128,512]{1,0,2:T(8,128)S(1)} %pad_maximum_fusion, f32[256,256]{1,0:T(8,128)S(1)} %copy-done.4, f32[256,256]{1,0:T(8,128)S(1)} %get-tuple-element.62), kind=kOutput, calls=%fused_computation.6 | convolution fusion | flops 12885032960 | bytes 25690112 | tf_op jit(solution)/shard_map/scm,mj->scj/dot_general | solution.py:140
  369.1 70.8 %reduce-scatter.2.cloned.1.call-done = f32[16,128,256]{2,1,0:T(8,128)} async-done(((f32[64,128,256]{2,1,0:T(8,128)}), f32[16,128,256]{2,1,0:T(8,128)}) %reduce-scatter.2.cloned.1.call-update) | async-done | bytes 2097168 | tf_op jit(solution)/shard_map/reduce_scatter | solution.py:139
  439.9 3.1 broadcast_multiply_fusion
  (39 shorter events, 11.1 us)
Async XLA Ops:
  6.5 280.1 %all-reduce.2.cloned.1.call-start = ((), (), s32[]{:S(2)}) async-start(), calls=%async_computation.1 | async-start | bytes 6291456 | tf_op jit(solution)/shard_map/psum | solution.py:124
  8.0 14.0 %copy-start.5 = (s32[4,16]{1,0:T(4,128)S(1)}, s32[4,16]{1,0:T(4,128)}, u32[]{:S(2)}) copy-start(s32[4,16]{1,0:T(4,128)} %param.13) | copy-start | bytes 772
  13.0 2.7 copy-start.3
  15.8 38.5 %collective-permute-start = (bf16[48,16,512]{2,1,0:T(8,128)(2,1)S(1)}, bf16[48,16,512]{2,1,0:T(8,128)(2,1)S(1)}, u32[]{:S(2)}, u32[]{:S(2)}) collective-permute-start(bf16[48,16,512]{2,1,0:T(8,128)(2,1)S(1)} %get-tuple-element.48), channel_id=1, source_target_pairs={{0,4},{4,8},{8,12},{12,16},{16,20},{20,24},{24,28},{1,5},{5,9},{9,... | collective-permute-start | bytes 2359304 | tf_op jit(solution)/shard_map/ppermute | solution.py:15
  20.7 33.6 %collective-permute-start.1 = (bf16[48,16,512]{2,1,0:T(8,128)(2,1)S(1)}, bf16[48,16,512]{2,1,0:T(8,128)(2,1)S(1)}, u32[]{:S(2)}, u32[]{:S(2)}) collective-permute-start(bf16[48,16,512]{2,1,0:T(8,128)(2,1)S(1)} %get-tuple-element.49), channel_id=1, source_target_pairs={{4,0},{8,4},{12,8},{16,12},{20,16},{24,20},{28,24},{5,1},{9,5},{13... | collective-permute-start | bytes 2359304 | tf_op jit(solution)/shard_map/ppermute | solution.py:18
  136.1 6.3 %copy-start = (bf16[6144,512]{1,0:T(8,128)(2,1)}, bf16[6144,512]{1,0:T(8,128)(2,1)S(1)}, u32[]{:S(2)}) copy-start(bf16[6144,512]{1,0:T(8,128)(2,1)S(1)} %fusion.2) | copy-start | bytes 18874372
  158.6 281.4 %reduce-scatter.2.cloned.1.call-start = ((), (), s32[]{:S(2)}) async-start(), calls=%async_computation.2 | async-start | bytes 10485760 | tf_op jit(solution)/shard_map/reduce_scatter | solution.py:139
  298.4 4.3 copy-start.1
  298.4 4.7 %copy-start.2 = (bf16[48,64,256]{1,0,2:T(8,128)(2,1)S(1)}, bf16[48,64,256]{1,0,2:T(8,128)(2,1)}, u32[]{:S(2)}) copy-start(bf16[48,64,256]{1,0,2:T(8,128)(2,1)} %copy.51) | copy-start | bytes 4718596
  319.6 7.2 %copy-start.4 = (f32[256,256]{1,0:T(8,128)S(1)}, f32[256,256]{1,0:T(8,128)}, u32[]{:S(2)}) copy-start(f32[256,256]{1,0:T(8,128)} %get-tuple-element.63) | copy-start | bytes 786436
Sparse Core Ops, SparseCore 0:
  158.7 127.8 all-reduce.1
  369.2 70.6 reduce-scatter.1
where the time goes:
time: 458 us; the launch traced here: 450 us
  waiting for transfers between devices  201 us (44%)
  matrix products  81.7 us (18%)
  local copies, waits for them, and re-layouts  53.7 us (12%)
  other arithmetic  48.3 us (11%)
  blocking collectives  34.4 us (8%)
  between operations  24.3 us (5%)
  starting transfers between devices  6.4 us (1%)
    psum x1, waiting for transfers between devices, per_device(): sources = lax.psum(offered_all.astype(jnp.bfloat16), 'fibre')  112 us
    reduce_scatter x1, waiting for transfers between devices, per_device(): lax.psum_scatter(jnp.einsum('scm,mj->scj', jnp.concatenate([real_sum, ima...  70.8 us
    dot_general x1, matrix products, per_device(): jnp.einsum('scm,mj->scj', jnp.concatenate([real_sum, imag_sum], axis=2),...  42.3 us
    all_gather x1, blocking collectives, entering(): gathered = lax.all_gather(part, axis)  34.4 us
    ppermute x1, waiting for transfers between devices, with_halo(): lax.ppermute(lax.slice_in_dim(block, block.shape[dim] - width, None, axis...  18.1 us
    another operation x1, other arithmetic, per_device(): local_cum = jnp.cumsum(detrended, axis=1)  15.4 us
    gather x4, local copies, waits for them, and re-layouts, per_device(): jnp.take(whitened, local_rows, axis=1)  13.5 us
    unnamed x14, local copies, waits for them, and re-layouts  11.4 us
  transfers between devices with their start and end apart: 4, of which 3 were waited for; matrix products, arithmetic and copies ran while one was open for 4% of the time, Pallas kernels for 0%

commit v1 on v0

--- a/solution.py
+++ b/solution.py
@@ -121,7 +121,7 @@
             )
         )
     offered_all = jnp.concatenate(offered, axis=1).astype(jnp.float32)
-    sources = lax.psum(offered_all.astype(jnp.bfloat16), "fibre")
+    sources = jnp.sum(lax.all_gather(offered_all.astype(jnp.bfloat16), "fibre"), axis=0)
     chan_re = whitened[:, :, :bin_count]
     chan_im = whitened[:, :, bin_count:]
     inverse = lag_table(length, bin_count, bin_count)

time: 458 us -> 828 us (1.81)
  waiting for transfers between devices: 201 us -> 554 us
  other arithmetic: 48.3 us -> 62.3 us
    all_gather x0 -> x1, waiting for transfers between devices: none -> 464 us  [per_device(): lax.all_gather(offered_all.astype(jnp.bfloat16), 'fibre')]
    psum x1 -> x0, waiting for transfers between devices: 112 us -> none  [per_device(): sources = lax.psum(offered_all.astype(jnp.bfloat16), 'fibre')]
    reduce_sum x0 -> x1, other arithmetic: none -> 14.1 us  [per_device(): jnp.sum(lax.all_gather(offered_all.astype(jnp.bfloat16), 'fibre'), axis=0)]
    unnamed x14 -> x16, local copies, waits for them, and re-layouts: 11.4 us -> 25 us
  transfers between devices with their start and end apart: 4 -> 4, of which waited for: 3 -> 3; matrix products, arithmetic and copies ran while one was open for 4% -> 2% of each run, Pallas kernels for 0% -> 0%
where the time goes in v1:
time: 828 us; the launch traced here: 821 us
  waiting for transfers between devices  554 us (67%)
  matrix products  81.7 us (10%)
  other arithmetic  62.3 us (8%)
  local copies, waits for them, and re-layouts  57.2 us (7%)
  blocking collectives  34.4 us (4%)
  between operations  24.3 us (3%)
    all_gather x1, waiting for transfers between devices, per_device(): lax.all_gather(offered_all.astype(jnp.bfloat16), 'fibre')  464 us
    reduce_scatter x1, waiting for transfers between devices, per_device(): lax.psum_scatter(jnp.einsum('scm,mj->scj', jnp.concatenate([real_sum, ima...  71.8 us
    dot_general x1, matrix products, per_device(): jnp.einsum('scm,mj->scj', jnp.concatenate([real_sum, imag_sum], axis=2),...  42.3 us
    all_gather x1, blocking collectives, entering(): gathered = lax.all_gather(part, axis)  34.4 us
    unnamed x16, local copies, waits for them, and re-layouts  25 us
    ppermute x1, waiting for transfers between devices, with_halo(): lax.ppermute(lax.slice_in_dim(block, block.shape[dim] - width, None, axis...  18.1 us
  transfers between devices with their start and end apart: 4, of which 3 were waited for; matrix products, arithmetic and copies ran while one was open for 2% of the time, Pallas kernels for 0%

profile of v1, /device:TPU:0, one launch (start us, length us, event | category | flops | bytes accessed | tf_op | source)
XLA Modules:
  0.0 820.5 jit_solution(4411301085426739968)
XLA Ops:
  8.0 5.0 fusion.3
  13.0 2.7 copy-done.3
  15.8 4.9 collective-permute-start
  33.1 3.0 multiply_convert_fusion
  36.1 18.1 %collective-permute-done = bf16[48,16,512]{2,1,0:T(8,128)(2,1)S(1)} collective-permute-done((bf16[48,16,512]{2,1,0:T(8,128)(2,1)S(1)}, bf16[48,16,512]{2,1,0:T(8,128)(2,1)S(1)}, u32[]{:S(2)}, u32[]{:S(2)}) %collective-permute-start) | collective-permute-done | bytes 786464 | tf_op jit(solution)/shard_map/ppermute | solution.py:15
  54.3 8.5 %bitcast_subtract_fusion = f32[48,128,512]{2,1,0:T(8,128)} fusion(bf16[48,128,512]{2,1,0:T(8,128)(2,1)} %copy-done.3, bf16[48,16,512]{2,1,0:T(8,128)(2,1)S(1)} %collective-permute-done.1, bf16[48,16,512]{2,1,0:T(8,128)(2,1)S(1)} %collective-permute-done), kind=kOutput, calls=%fused_computation.12 | convolution fusion | flops 1039745024 | bytes 20447232 | tf_op jit(solution)/shard_map/ck,skl->scl/dot_general | solution.py:89
  62.8 15.4 %fusion.4 = f32[48,128,512]{2,0,1:T(8,128)} fusion(f32[48,128,512]{2,1,0:T(8,128)} %bitcast_subtract_fusion), kind=kOutput, calls=%fused_computation.13 | output fusion | flops 399507456 | bytes 25165824 | tf_op jit(solution)/shard_map/jit(cumsum)/reduce_window_sum | solution.py:91
  79.0 34.4 %all-gather = f32[384,1,512]{2,0,1:T(8,128)S(1)} all-gather(f32[48,1,512]{2,0,1:T(8,128)S(1)} %slice.78), channel_id=2, replica_groups=mesh['fibre'=8,'day'=4] {'fibre'}, dimensions={0}, use_global_device_ids=true | all-gather | bytes 884736 | tf_op jit(solution)/shard_map/all_gather | solution.py:25
  113.7 6.6 add_convert_fusion
  120.3 3.6 copy.32
  123.9 4.4 fusion.20
  128.3 5.7 fusion.6
  134.0 2.0 fusion.2
  136.1 6.3 copy.35
  142.4 3.4 gather_fusion.3
  145.8 3.4 gather_fusion.2
  149.2 3.4 gather_fusion.1
  152.6 3.4 gather_fusion
  160.6 5.2 fusion.54
  165.8 5.0 copy.45
  170.8 3.4 copy.47
  174.2 464.0 %all-gather.4.cloned.1.call-done = bf16[384,64,512]{2,0,1:T(8,128)(2,1)} async-done(((bf16[48,64,512]{2,0,1:T(8,128)(2,1)}), bf16[384,64,512]{2,0,1:T(8,128)(2,1)}) %all-gather.4.cloned.1.call-update) | async-done | bytes 25165840 | tf_op jit(solution)/shard_map/all_gather | solution.py:124
  638.2 14.1 %reduce_sum.32 = bf16[48,64,512]{2,0,1:T(8,128)(2,1)S(1)} reduce(bf16[8,48,64,512]{3,1,0,2:T(8,128)(2,1)} %bitcast.59, bf16[]{:T(256)} %constant.119.clone.1), dimensions={0}, to_apply=%region_5.7 | reduce | flops 11010048 | bytes 28311554 | tf_op jit(solution)/shard_map/reduce_sum | solution.py:124
  654.2 6.8 copy.46
  661.0 6.7 copy.48
  667.7 4.3 fusion.58
  673.8 7.6 add_bitcast_fusion
  681.3 7.6 subtract_bitcast_fusion
  688.9 7.2 pad_maximum_fusion
  696.1 42.3 %fusion = f32[64,128,256]{2,1,0:T(8,128)} fusion(f32[64,128,512]{1,0,2:T(8,128)S(1)} %pad_maximum_fusion, f32[256,256]{1,0:T(8,128)S(1)} %copy-done.4, f32[256,256]{1,0:T(8,128)S(1)} %get-tuple-element.62), kind=kOutput, calls=%fused_computation.6 | convolution fusion | flops 12885032960 | bytes 25690112 | tf_op jit(solution)/shard_map/scm,mj->scj/dot_general | solution.py:140
  738.4 71.8 %reduce-scatter.2.cloned.1.call-done = f32[16,128,256]{2,1,0:T(8,128)} async-done(((f32[64,128,256]{2,1,0:T(8,128)}), f32[16,128,256]{2,1,0:T(8,128)}) %reduce-scatter.2.cloned.1.call-update) | async-done | bytes 2097168 | tf_op jit(solution)/shard_map/reduce_scatter | solution.py:139
  810.2 3.1 broadcast_multiply_fusion
  (40 shorter events, 12.9 us)
Async XLA Ops:
  6.5 631.6 %all-gather.4.cloned.1.call-start = ((), (), s32[]{:S(2)}) async-start(), calls=%async_computation.2 | async-start | bytes 28311552 | tf_op jit(solution)/shard_map/all_gather | solution.py:124
  8.0 14.0 %copy-start.5 = (s32[4,16]{1,0:T(4,128)S(1)}, s32[4,16]{1,0:T(4,128)}, u32[]{:S(2)}) copy-start(s32[4,16]{1,0:T(4,128)} %param.13) | copy-start | bytes 772
  13.0 2.7 copy-start.3
  15.8 38.5 %collective-permute-start = (bf16[48,16,512]{2,1,0:T(8,128)(2,1)S(1)}, bf16[48,16,512]{2,1,0:T(8,128)(2,1)S(1)}, u32[]{:S(2)}, u32[]{:S(2)}) collective-permute-start(bf16[48,16,512]{2,1,0:T(8,128)(2,1)S(1)} %get-tuple-element.48), channel_id=1, source_target_pairs={{0,4},{4,8},{8,12},{12,16},{16,20},{20,24},{24,28},{1,5},{5,9},{9,... | collective-permute-start | bytes 2359304 | tf_op jit(solution)/shard_map/ppermute | solution.py:15
  20.7 33.6 %collective-permute-start.1 = (bf16[48,16,512]{2,1,0:T(8,128)(2,1)S(1)}, bf16[48,16,512]{2,1,0:T(8,128)(2,1)S(1)}, u32[]{:S(2)}, u32[]{:S(2)}) collective-permute-start(bf16[48,16,512]{2,1,0:T(8,128)(2,1)S(1)} %get-tuple-element.49), channel_id=1, source_target_pairs={{4,0},{8,4},{12,8},{16,12},{20,16},{24,20},{28,24},{5,1},{9,5},{13... | collective-permute-start | bytes 2359304 | tf_op jit(solution)/shard_map/ppermute | solution.py:18
  136.1 6.3 copy-start
  158.5 651.7 %reduce-scatter.2.cloned.1.call-start = ((), (), s32[]{:S(2)}) async-start(), calls=%async_computation.1 | async-start | bytes 10485760 | tf_op jit(solution)/shard_map/reduce_scatter | solution.py:139
  667.7 4.3 copy-start.1
  667.7 4.7 copy-start.2
  688.9 7.2 copy-start.4
Sparse Core Ops, SparseCore 0:
  158.6 479.4 all-gather.3
  738.5 71.6 reduce-scatter.1
